TPU v7x, 32 devices: a whole 2x2x4 slice. The times are simulated.
32 devices in a mesh: groups: 1, expert: 8 (over z, core), dp: 4 (over y, x).
Axes of the slice: x: 2, y: 2, z: 4, core: 2. Of those that a mesh axis runs over, the one named last changes fastest.
Arguments:
- tokens: bfloat16 [128, 4096], P(('groups', 'expert', 'dp')), may hold values from -6 to 6
- expert_ids: int32 [128, 2], P(('groups', 'expert', 'dp')), may hold values from 0 to 7, as said below
- gate_weights: bfloat16 [128, 2], P(('groups', 'expert', 'dp')), may hold values from 0.099609375 to 1
- placement: int32 [2, 2], P('groups'), may hold values from 0 to 7, as said below
- w_gate: bfloat16 [8, 1536, 4096], P('expert', 'dp'), may hold values from -0.09375 to 0.09375
- w_up: bfloat16 [8, 1536, 4096], P('expert', 'dp'), may hold values from -0.09375 to 0.09375
- w_down: bfloat16 [8, 1536, 4096], P('expert', 'dp'), may hold values from -0.15625 to 0.15625
Outputs:
- mixed: bfloat16 [128, 4096], P(('groups', 'expert', 'dp'))
Inputs may be any that keep to these rules, and one draw needn't show every extreme that they name: `expert_ids`: each row names 2 different experts. In each aligned block of 16 rows (the tokens of one index of expert) no expert is named by more than 6 rows, and some expert is named by exactly that many. `placement`: row 0 holds 2 different experts; row 1 holds 2 different expert indices, none of which appears in row 0.
All inputs are finite; a program needn't handle non-finite values.
Results may differ from a plain program's by a relative error of at most 0.015.
Values may be sent and summed in bfloat16 or wider, within the bound.
A program may use at most 64 MiB of HBM per device.

v0:
```python
import jax
import jax.numpy as jnp
from jax import lax
from jax.sharding import PartitionSpec as P


def expert_block(rows, gate_w, up_w, down_w):
    contract = (((1,), (1,)), ((), ()))
    gate = lax.dot_general(rows, gate_w, contract, preferred_element_type=jnp.float32)
    up = lax.dot_general(rows, up_w, contract, preferred_element_type=jnp.float32)
    hidden = (jax.nn.silu(gate) * up).astype(jnp.bfloat16)
    return jnp.dot(hidden, down_w, preferred_element_type=jnp.float32).astype(jnp.bfloat16)


def body(tokens, expert_ids, gate_weights, placement, w_gate, w_up, w_down):
    group_source, group_gates = (
        lax.all_gather(tokens, "dp", axis=0, tiled=True),
        lax.all_gather(gate_weights, "dp", axis=0, tiled=True),
    )
    group_ids = lax.all_gather(expert_ids, "dp", axis=0, tiled=True)
    experts = lax.axis_size("expert")
    my_index = lax.axis_index("expert")
    width = tokens.shape[1]
    group = group_ids.shape[0]
    topk = expert_ids.shape[1]
    first = max(2, group * topk // experts)
    second = max(1, first // 2)
    slots = first + second
    pair_ids = group_ids.reshape(-1)
    onehot = (pair_ids[:, None] == jnp.arange(experts, dtype=jnp.int32)[None, :]).astype(jnp.int32)
    rank = jnp.sum((jnp.cumsum(onehot, axis=0) - onehot) * onehot, axis=1)
    match = pair_ids[:, None] == placement[0][None, :]
    listed = jnp.any(match, axis=1)
    keep = (rank < first) | listed & (rank < slots)
    dest = jnp.where(keep, pair_ids * slots + rank, -1)
    row_iota = jnp.arange(experts * slots, dtype=jnp.int32)
    pick = (dest[None, :] == row_iota[:, None]).reshape(experts * slots, group, topk)
    select = jnp.any(pick, axis=2).astype(jnp.bfloat16)
    weights_rows = jnp.sum(
        jnp.where(pick, group_gates[None, :, :].astype(jnp.float32), 0.0), axis=2
    ).astype(jnp.bfloat16)
    send = jnp.dot(select, group_source, preferred_element_type=jnp.float32).astype(jnp.bfloat16)
    received = lax.all_to_all(
        send.reshape(experts, slots, width), "expert", split_axis=0, concat_axis=0, tiled=True
    )
    main = expert_block(received[:, :first].reshape(-1, width), w_gate[0], w_up[0], w_down[0])
    active = jnp.any(placement[0] == my_index)
    extra_weights = (w_gate[0], w_up[0], w_down[0])
    extra_rows = received[:, first:].reshape(-1, width)
    extra = lax.cond(
        active,
        lambda: expert_block(extra_rows, extra_weights[0], extra_weights[1], extra_weights[2]),
        lambda: jnp.zeros((experts * second, width), jnp.bfloat16),
    )
    partial_value = jnp.concatenate(
        [main.reshape(experts, first, width), extra.reshape(experts, second, width)], axis=1
    )
    contract = (((0,), (0,)), ((), ()))
    summed = lax.psum_scatter(
        partial_value.astype(jnp.float32).astype(jnp.bfloat16),
        "dp",
        scatter_dimension=2,
        tiled=True,
    ).astype(jnp.float32)
    back = lax.all_to_all(
        summed.astype(jnp.bfloat16), "expert", split_axis=0, concat_axis=0, tiled=True
    ).astype(summed.dtype)
    group_cols = lax.dot_general(
        weights_rows.astype(jnp.float32),
        back.reshape(experts * slots, -1),
        contract,
        precision=lax.Precision.HIGHEST,
        preferred_element_type=jnp.float32,
    )
    mine_out = lax.all_to_all(
        group_cols.astype(jnp.bfloat16), "dp", split_axis=0, concat_axis=1, tiled=True
    ).astype(group_cols.dtype)
    return mine_out.astype(jnp.bfloat16)


def solution(mesh):
    placed = (
        P(("groups", "expert", "dp"), None),
        P(("groups", "expert", "dp"), None),
        P(("groups", "expert", "dp"), None),
        P("groups", None),
        P("expert", "dp", None),
        P("expert", "dp", None),
        P("expert", "dp", None),
    )
    return jax.shard_map(
        body,
        mesh=mesh,
        in_specs=placed,
        out_specs=P(("groups", "expert", "dp"), None),
        check_vma=False,
    )
```

profile of v0, /device:TPU:0, one launch (start us, length us, event | category | flops | bytes accessed | tf_op | source)
XLA Modules:
  0.0 121.4 jit_solution(14547632915415462673)
XLA Ops:
  6.5 9.9 %all-gather = s32[4,4,2]{1,2,0:T(2,128)S(1)} all-gather(s32[1,4,2]{1,2,0:T(2,128)} %bitcast.40), channel_id=1, replica_groups=mesh['groups'=1,'expert'=8,'dp'=4] {'dp'}, dimensions={0}, use_global_device_ids=true | all-gather | bytes 160 | tf_op jit(solution)/shard_map/all_gather | solution.py:20
  16.9 0.2 select_reduce_fusion.1
  17.2 0.7 slice_bitcast_fusion
  18.3 8.3 %all-gather.2 = bf16[4,4,4096]{2,1,0:T(4,128)(2,1)S(1)} all-gather(bf16[1,4,4096]{2,1,0:T(4,128)(2,1)} %bitcast.38), channel_id=1, replica_groups=mesh['groups'=1,'expert'=8,'dp'=4] {'dp'}, dimensions={0}, use_global_device_ids=true | all-gather | bytes 163840 | tf_op jit(solution)/shard_map/all_gather | solution.py:17
  26.6 0.7 reshape.64
  27.2 1.2 convolution_convert_fusion.1
  28.5 0.9 reshape.55
  29.4 4.9 %all-to-all-start = ((bf16[8,6,4096]{2,1,0:T(8,128)(2,1)}), bf16[8,6,4096]{2,1,0:T(8,128)(2,1)}, u32[]{:S(2)}, u32[]{:S(2)}) async-start(bf16[8,6,4096]{2,1,0:T(8,128)(2,1)} %reshape.55), calls=%async_computation | async-start | bytes 1048576 | tf_op jit(solution)/shard_map/all_to_all | solution.py:43
  34.3 1.3 %compare_reduce_fusion = pred[]{:T(512)} fusion(s32[]{:T(128)S(6)} %axis_index.15, s32[2,2]{1,0:T(2,128)} %param.12), kind=kLoop, calls=%fused_computation.32 | loop fusion | flops 3 | bytes 13 | tf_op jit(solution)/shard_map/reduce_or | solution.py:47
  36.3 13.4 %all-to-all-done = bf16[8,6,4096]{2,1,0:T(8,128)(2,1)} async-done(((bf16[8,6,4096]{2,1,0:T(8,128)(2,1)}), bf16[8,6,4096]{2,1,0:T(8,128)(2,1)}, u32[]{:S(2)}, u32[]{:S(2)}) %all-to-all-start) | async-done | bytes 393248 | tf_op jit(solution)/shard_map/all_to_all | solution.py:43
  49.7 1.8 %slice.13 = bf16[8,4,4096]{2,1,0:T(4,128)(2,1)} slice(bf16[8,6,4096]{2,1,0:T(8,128)(2,1)} %all-to-all-done), slice={[0:8], [0:4], [0:4096]} | slice | bytes 524288 | tf_op jit(solution)/shard_map/slice | solution.py:46
  51.5 1.0 reshape.56
  52.6 1.0 fusion.21
  53.6 5.6 %convolution_convert_fusion.2 = bf16[32,4096]{1,0:T(8,128)(2,1)} fusion(bf16[32,4096]{1,0:T(8,128)(2,1)S(1)} %reshape.56, f32[32,384]{1,0:T(8,128)S(1)} %fusion.21, bf16[1,384,4096]{2,1,0:T(8,128)(2,1)} %param.15, bf16[1,384,4096]{2,1,0:T(8,128)(2,1)} %param.14), kind=kOutput, calls=%fused_computation.11 | convolution fusion | flops 201531392 | bytes 6864896 | tf_op jit(solution)/shard_map/dot_general | solution.py:12
  59.2 1.1 reshape.57
  60.3 0.7 conditional.1
  60.3 0.7 reshape.48
  61.0 1.9 %pad_maximum_fusion = bf16[8,6,4096]{2,1,0:T(8,128)(2,1)} fusion(bf16[8,2,4096]{2,1,0:T(2,128)(2,1)} %get-tuple-element.23, bf16[8,4,4096]{2,1,0:T(4,128)(2,1)S(1)} %reshape.57), kind=kLoop, calls=%fused_computation.15 | loop fusion | flops 786432 | bytes 786432 | tf_op jit(solution)/shard_map/concatenate | solution.py:55
  63.0 7.2 %all-gather.1 = bf16[4,4,2]{1,2,0:T(2,128)(2,1)S(1)} all-gather(bf16[1,4,2]{1,2,0:T(2,128)(2,1)S(1)} %bitcast.41), channel_id=1, replica_groups=mesh['groups'=1,'expert'=8,'dp'=4] {'dp'}, dimensions={0}, use_global_device_ids=true | all-gather | bytes 80 | tf_op jit(solution)/shard_map/all_gather | solution.py:18
  70.2 24.9 %reduce-scatter.2.cloned.1.call-done = bf16[8,6,1024]{2,1,0:T(8,128)(2,1)} async-done(((bf16[8,6,4096]{2,1,0:T(8,128)(2,1)}), bf16[8,6,1024]{2,1,0:T(8,128)(2,1)}) %reduce-scatter.2.cloned.1.call-update) | async-done | bytes 98320 | tf_op jit(solution)/shard_map/reduce_scatter | solution.py:59
  95.1 4.6 %all-to-all-start.1 = ((bf16[8,6,1024]{2,1,0:T(8,128)(2,1)}), bf16[8,6,1024]{2,1,0:T(8,128)(2,1)S(1)}, u32[]{:S(2)}, u32[]{:S(2)}) async-start(bf16[8,6,1024]{2,1,0:T(8,128)(2,1)} %reduce-scatter.2.cloned.1.call-done), calls=%async_computation.2 | async-start | bytes 262144 | tf_op jit(solution)/shard_map/all_to_all | solution.py:65
  99.9 6.6 %all-to-all-done.1 = bf16[8,6,1024]{2,1,0:T(8,128)(2,1)S(1)} async-done(((bf16[8,6,1024]{2,1,0:T(8,128)(2,1)}), bf16[8,6,1024]{2,1,0:T(8,128)(2,1)S(1)}, u32[]{:S(2)}, u32[]{:S(2)}) %all-to-all-start.1) | async-done | bytes 98336 | tf_op jit(solution)/shard_map/all_to_all | solution.py:65
  106.6 7.3 %all_to_all.29 = bf16[4,4,1024]{2,1,0:T(4,128)(2,1)S(1)} all-to-all(bf16[4,4,1024]{2,1,0:T(4,128)(2,1)S(1)} %all_to_all.22), channel_id=1, replica_groups=mesh['groups'=1,'expert'=8,'dp'=4] {'dp'}, dimensions={0} | all-to-all | bytes 65536 | tf_op jit(solution)/shard_map/all_to_all | solution.py:75
  113.9 0.6 copy.44
  (24 shorter events, 1.3 us)
Async XLA Ops:
  6.5 46.0 %copy-start = (bf16[1,384,4096]{2,1,0:T(8,128)(2,1)S(1)}, bf16[1,384,4096]{2,1,0:T(8,128)(2,1)}, u32[]{:S(2)}) copy-start(bf16[1,384,4096]{2,1,0:T(8,128)(2,1)} %param.13) | copy-start | bytes 9437188
  29.4 20.3 %all-to-all-start = ((bf16[8,6,4096]{2,1,0:T(8,128)(2,1)}), bf16[8,6,4096]{2,1,0:T(8,128)(2,1)}, u32[]{:S(2)}, u32[]{:S(2)}) async-start(bf16[8,6,4096]{2,1,0:T(8,128)(2,1)} %reshape.55), calls=%async_computation | async-start | bytes 1048576 | tf_op jit(solution)/shard_map/all_to_all | solution.py:43
  34.3 60.8 %reduce-scatter.2.cloned.1.call-start = ((), (), s32[]{:S(2)}) async-start(), calls=%async_computation.4 | async-start | bytes 655360 | tf_op jit(solution)/shard_map/reduce_scatter | solution.py:59
  60.2 2.7 %copy-start.1 = (bf16[4,2]{0,1:T(2,128)(2,1)S(1)}, bf16[4,2]{0,1:T(2,128)(2,1)}, u32[]{:S(2)}) copy-start(bf16[4,2]{0,1:T(2,128)(2,1)} %param.11) | copy-start | bytes 52
  95.1 11.4 %all-to-all-start.1 = ((bf16[8,6,1024]{2,1,0:T(8,128)(2,1)}), bf16[8,6,1024]{2,1,0:T(8,128)(2,1)S(1)}, u32[]{:S(2)}, u32[]{:S(2)}) async-start(bf16[8,6,1024]{2,1,0:T(8,128)(2,1)} %reduce-scatter.2.cloned.1.call-done), calls=%async_computation.2 | async-start | bytes 262144 | tf_op jit(solution)/shard_map/all_to_all | solution.py:65
Sparse Core Ops, SparseCore 0:
  63.1 31.9 reduce-scatter.1
where the time goes:
time: 122 us; the launch traced here: 121 us
  waiting for transfers between devices  44.9 us (37%)
  blocking collectives  32.7 us (27%)
  between operations  14.1 us (12%)
  starting transfers between devices  9.52 us (8%)
  local copies, waits for them, and re-layouts  8.28 us (7%)
  matrix products  7.95 us (7%)
  other arithmetic  3.84 us (3%)
    reduce_scatter x1, waiting for transfers between devices, body(): lax.psum_scatter(partial_value.astype(jnp.float32).astype(jnp.bfloat16),...  24.9 us
    all_to_all x1, waiting for transfers between devices, body(): lax.all_to_all(send.reshape(experts, slots, width), 'expert', split_axis=...  13.4 us
    all_gather x1, blocking collectives, body(): group_ids = lax.all_gather(expert_ids, 'dp', axis=0, tiled=True)  9.95 us
    all_gather x1, blocking collectives, body(): lax.all_gather(tokens, 'dp', axis=0, tiled=True)  8.3 us
    all_to_all x1, blocking collectives, body(): lax.all_to_all(group_cols.astype(jnp.bfloat16), 'dp', split_axis=0, conca...  7.3 us
    all_gather x1, blocking collectives, body(): lax.all_gather(gate_weights, 'dp', axis=0, tiled=True)  7.17 us
    all_to_all x1, waiting for transfers between devices, body(): lax.all_to_all(summed.astype(jnp.bfloat16), 'expert', split_axis=0, conca...  6.58 us
    dot_general x1, matrix products, expert_block(): jnp.dot(hidden, down_w, preferred_element_type=jnp.float32)  5.59 us
  transfers between devices with their start and end apart: 3, of which 3 were waited for; matrix products, arithmetic and copies ran while one was open for 1% of the time, Pallas kernels for 0%

commit v1 on v0

v1 whole, which is shorter than its diff:
```python
import functools

import jax
import jax.numpy as jnp
from jax import lax
from jax.experimental import pallas as pl
from jax.experimental.pallas import tpu as pltpu
from jax.sharding import PartitionSpec as P

MESH = pl.DeviceIdType.MESH
F32 = jnp.float32
BF16 = jnp.bfloat16


def each(count, step):
    if count <= 8:
        for i in range(count):
            step(i)
    else:
        def turn(i, carry):
            step(i)
            return carry

        lax.fori_loop(0, count, turn, 0)


def each_from(first, count, step):
    each(count - first, lambda i: step(i + first))


def kernel(experts, dp, topk, first, slots, padded,
           tok, ids, gates, placement, wg_hbm, wu_hbm, wd_hbm, out,
           wg, wu, wd, tok_s, tok_r, info_s, info_r, group_x, disp_s, rows_r, rows_f, part_f,
           part_s, part_r, back_s, back_r, wsel, mix_s, mix_r,
           w_sem, s1, r1, si, ri, s2, r2, s3, r3, s4, r4, s5, r5, s6, r6):
    me_e = lax.axis_index("expert")
    me_j = lax.axis_index("dp")
    own, width = tok.shape
    block = width // dp
    group = own * dp
    pairs = group * topk
    lanes = info_s.shape[1]
    total = experts * padded

    loads = [pltpu.make_async_copy(a, b, w_sem.at[i])
             for i, (a, b) in enumerate(((wg_hbm, wg), (wu_hbm, wu), (wd_hbm, wd)))]
    for load in loads:
        load.start()

    def to_dp(src, dst, send, recv, shift):
        return pltpu.make_async_remote_copy(
            src_ref=src, dst_ref=dst, send_sem=send, recv_sem=recv,
            device_id={"dp": lax.rem(me_j + shift, dp)}, device_id_type=MESH)

    def to_expert(src, dst, send, recv, shift):
        return pltpu.make_async_remote_copy(
            src_ref=src, dst_ref=dst, send_sem=send, recv_sem=recv,
            device_id={"expert": lax.rem(me_e + shift, experts)}, device_id_type=MESH)

    def cols(j):
        return pl.ds(pl.multiple_of(j * block, 128), block)

    barrier = pltpu.get_barrier_semaphore()
    for s in range(1, dp):
        pl.semaphore_signal(barrier, inc=1, device_id={"dp": lax.rem(me_j + s, dp)}, device_id_type=MESH)

    def greet(d):
        pl.semaphore_signal(barrier, inc=1, device_id={"expert": lax.rem(me_e + d, experts)}, device_id_type=MESH)

    each_from(1, experts, greet)

    lane = lax.broadcasted_iota(jnp.int32, (8, lanes), 1)
    line = lax.broadcasted_iota(jnp.int32, (8, lanes), 0)
    id_f = ids[...].astype(F32)
    gate_f = gates[...].astype(F32)
    info = jnp.zeros((8, lanes), F32)
    for t in range(own):
        for k in range(topk):
            here = lane == (me_j * own + t) * topk + k
            value = jnp.where(line == 0, jnp.broadcast_to(id_f[t:t + 1, k:k + 1], (8, lanes)),
                              jnp.broadcast_to(gate_f[t:t + 1, k:k + 1], (8, lanes)))
            info = jnp.where(here, value, info)
    info_s[...] = info
    for s in range(1, dp):
        tok_s[s] = tok[:, cols(lax.rem(me_j + s, dp))]
    tok_r[me_j] = tok[:, cols(me_j)]

    pl.semaphore_wait(barrier, dp - 1 + experts - 1)

    for s in range(1, dp):
        to_dp(info_s, info_r.at[s], si.at[s], ri.at[s], s).start()
    for s in range(1, dp):
        to_dp(tok_s.at[s], tok_r.at[me_j], s1.at[s], r1.at[s], s).start()
    for s in range(1, dp):
        to_dp(info_s, info_r.at[s], si.at[s], ri.at[s], s).wait_recv()
        info = info + info_r[s]

    id_row = info[0:1, :]
    gate_row = info[1:2, :]
    at_row = lax.broadcasted_iota(jnp.int32, (pairs, lanes), 0)
    at_lane = lax.broadcasted_iota(jnp.int32, (pairs, lanes), 1)
    id_col = jnp.sum(jnp.where(at_row == at_lane, jnp.broadcast_to(id_row, (pairs, lanes)), 0.0),
                     axis=1, keepdims=True)
    same = jnp.broadcast_to(id_col, (pairs, lanes)) == jnp.broadcast_to(id_row, (pairs, lanes))
    rank = jnp.sum(jnp.where(same, jnp.where(at_row < at_lane, 1.0, 0.0), 0.0), axis=0, keepdims=True)
    limit = jnp.full((1, lanes), float(first), F32)
    for h in range(placement.shape[1]):
        limit = jnp.where(id_row == placement[0, h].astype(F32), float(slots), limit)
    dest = jnp.where(rank < limit, id_row * float(padded) + rank, -1.0)
    dest = jnp.where(lax.broadcasted_iota(jnp.int32, (1, lanes), 1) < pairs, dest, -1.0)
    pick = lax.broadcasted_iota(jnp.int32, (total, lanes), 0).astype(F32) == jnp.broadcast_to(dest, (total, lanes))
    pair_i = lax.broadcasted_iota(jnp.int32, (lanes, group), 0)
    token_i = lax.broadcasted_iota(jnp.int32, (lanes, group), 1) * topk
    fold = jnp.where(pair_i >= token_i, jnp.where(pair_i < token_i + topk, 1.0, 0.0), 0.0).astype(BF16)
    select = jnp.dot(jnp.where(pick, 1.0, 0.0).astype(BF16), fold, preferred_element_type=F32).astype(BF16)
    wsel[...] = jnp.dot(jnp.where(pick, jnp.broadcast_to(gate_row, (total, lanes)), 0.0).astype(BF16), fold,
                        preferred_element_type=F32)

    for s in range(1, dp):
        to_dp(tok_s.at[s], tok_r.at[lax.rem(me_j + dp - s, dp)], s1.at[s], r1.at[s], s).wait_recv()
    for j in range(dp):
        group_x[j * own:(j + 1) * own, :] = tok_r[j].astype(F32)
    rows_f[...] = jnp.dot(select, group_x[...].astype(BF16), preferred_element_type=F32)

    def dispatch(d):
        e = lax.rem(me_e + d, experts)
        start = pl.multiple_of(e * padded, 8)
        disp_s[e] = rows_f[pl.ds(start, slots), :].astype(BF16)
        to_expert(disp_s.at[e], rows_r.at[me_j, me_e], s2.at[d], r2.at[d], d).start()

    each_from(1, experts, dispatch)
    rows_r[me_j, me_e] = rows_f[pl.ds(pl.multiple_of(me_e * padded, 8), slots), :].astype(BF16)

    def forward(d):
        g = lax.rem(me_e + experts - d, experts)
        for s in range(1, dp):
            to_dp(rows_r.at[me_j, g], rows_r.at[me_j, g], s3.at[s, d], r3.at[s, d], s).start()

    forward(0)

    def arrive(d):
        g = lax.rem(me_e + experts - d, experts)
        to_expert(disp_s.at[g], rows_r.at[me_j, g], s2.at[d], r2.at[d], d).wait_recv()
        forward(d)

    each_from(1, experts, arrive)

    loads[0].wait()
    loads[1].wait()
    contract = (((1,), (1,)), ((), ()))
    gate = up = None
    for s in range(dp):
        j = lax.rem(me_j + dp - s, dp)

        def take(d):
            g = lax.rem(me_e + experts - d, experts)
            if s > 0:
                to_dp(rows_r.at[j, g], rows_r.at[j, g], s3.at[s, d], r3.at[s, d], s).wait_recv()
            rows_f[pl.ds(pl.multiple_of(g * padded, 8), slots), :] = rows_r[j, g].astype(F32)

        each(experts, take)
        x = rows_f[...].astype(BF16)
        gate_part = lax.dot_general(x, wg[:, cols(j)], contract, preferred_element_type=F32)
        up_part = lax.dot_general(x, wu[:, cols(j)], contract, preferred_element_type=F32)
        gate = gate_part if gate is None else gate + gate_part
        up = up_part if up is None else up + up_part
    hidden = (gate / (1.0 + jnp.exp(-gate)) * up).astype(BF16)

    loads[2].wait()
    for s in list(range(1, dp)) + [0]:
        j = lax.rem(me_j + s, dp)
        part_f[...] = jnp.dot(hidden, wd[:, cols(j)], preferred_element_type=F32)
        target = part_s if s > 0 else part_r

        def split(g):
            target[s, g] = part_f[pl.ds(g * padded, slots), :].astype(BF16)

        each(experts, split)
        if s > 0:
            to_dp(part_s.at[s], part_r.at[s], s4.at[s], r4.at[s], s).start()
    for s in range(1, dp):
        to_dp(part_s.at[s], part_r.at[s], s4.at[s], r4.at[s], s).wait_recv()

    def summed(g):
        value = part_r[0, g].astype(F32)
        for s in range(1, dp):
            value = value + part_r[s, g].astype(F32)
        return value.astype(BF16)

    def give(d):
        g = lax.rem(me_e + d, experts)
        back_s[g] = summed(g)
        to_expert(back_s.at[g], back_r.at[me_e], s5.at[d], r5.at[d], d).start()

    each_from(1, experts, give)
    back_r[me_e] = summed(me_e)

    def collect(d):
        e = lax.rem(me_e + experts - d, experts)
        to_expert(back_s.at[e], back_r.at[e], s5.at[d], r5.at[d], d).wait_recv()

    each_from(1, experts, collect)

    def place(e):
        rows_f[pl.ds(e * padded, slots), :] = back_r[e].astype(F32)

    each(experts, place)
    group_x[...] = lax.dot_general(wsel[...].astype(BF16), rows_f[...].astype(BF16), (((0,), (0,)), ((), ())),
                                   preferred_element_type=F32)
    for j in range(dp):
        mix_s[j] = group_x[j * own:(j + 1) * own, :].astype(BF16)
    for s in range(1, dp):
        to_dp(mix_s.at[lax.rem(me_j + s, dp)], mix_r.at[me_j], s6.at[s], r6.at[s], s).start()
    mix_r[me_j] = mix_s[me_j]
    for s in range(1, dp):
        j = lax.rem(me_j + dp - s, dp)
        to_dp(mix_s.at[j], mix_r.at[j], s6.at[s], r6.at[s], s).wait_recv()
    for j in range(dp):
        out[:, j * block:(j + 1) * block] = mix_r[j]

    for s in range(1, dp):
        to_dp(info_s, info_r.at[s], si.at[s], ri.at[s], s).wait_send()
        to_dp(tok_s.at[s], tok_r.at[me_j], s1.at[s], r1.at[s], s).wait_send()
        to_dp(part_s.at[s], part_r.at[s], s4.at[s], r4.at[s], s).wait_send()
        to_dp(mix_s.at[lax.rem(me_j + s, dp)], mix_r.at[me_j], s6.at[s], r6.at[s], s).wait_send()

    def left(d):
        g = lax.rem(me_e + experts - d, experts)
        for s in range(1, dp):
            to_dp(rows_r.at[me_j, g], rows_r.at[me_j, g], s3.at[s, d], r3.at[s, d], s).wait_send()

    def left_expert(d):
        e = lax.rem(me_e + d, experts)
        to_expert(disp_s.at[e], rows_r.at[me_j, me_e], s2.at[d], r2.at[d], d).wait_send()
        to_expert(back_s.at[e], back_r.at[me_e], s5.at[d], r5.at[d], d).wait_send()

    each(experts, left)
    each_from(1, experts, left_expert)


def body(tokens, expert_ids, gate_weights, placement, w_gate, w_up, w_down):
    experts = lax.axis_size("expert")
    dp = lax.axis_size("dp")
    own, width = tokens.shape
    topk = expert_ids.shape[1]
    group = own * dp
    first = max(2, group * topk // experts)
    slots = first + max(1, first // 2)
    padded = -(-slots // 8) * 8
    lanes = -(-group * topk // 128) * 128
    block = width // dp
    units = w_gate.shape[1]
    total = experts * padded
    vmem = pl.BlockSpec(memory_space=pltpu.VMEM)
    smem = pl.BlockSpec(memory_space=pltpu.SMEM)
    hbm = pl.BlockSpec(memory_space=pl.ANY)
    dma = pltpu.SemaphoreType.DMA
    return pl.pallas_call(
        functools.partial(kernel, experts, dp, topk, first, slots, padded),
        out_shape=jax.ShapeDtypeStruct((own, width), BF16),
        in_specs=[vmem, vmem, vmem, smem, hbm, hbm, hbm],
        out_specs=vmem,
        scratch_shapes=[
            pltpu.VMEM((units, width), BF16),
            pltpu.VMEM((units, width), BF16),
            pltpu.VMEM((units, width), BF16),
            pltpu.VMEM((dp, own, block), BF16),
            pltpu.VMEM((dp, own, block), BF16),
            pltpu.VMEM((8, lanes), F32),
            pltpu.VMEM((dp, 8, lanes), F32),
            pltpu.VMEM((group, block), F32),
            pltpu.VMEM((experts, slots, block), BF16),
            pltpu.VMEM((dp, experts, slots, block), BF16),
            pltpu.VMEM((total, block), F32),
            pltpu.VMEM((total, block), F32),
            pltpu.VMEM((dp, experts, slots, block), BF16),
            pltpu.VMEM((dp, experts, slots, block), BF16),
            pltpu.VMEM((experts, slots, block), BF16),
            pltpu.VMEM((experts, slots, block), BF16),
            pltpu.VMEM((total, group), F32),
            pltpu.VMEM((dp, own, block), BF16),
            pltpu.VMEM((dp, own, block), BF16),
            dma((3,)),
            dma((dp,)), dma((dp,)), dma((dp,)), dma((dp,)),
            dma((experts,)), dma((experts,)),
            dma((dp, experts)), dma((dp, experts)),
            dma((dp,)), dma((dp,)),
            dma((experts,)), dma((experts,)),
            dma((dp,)), dma((dp,)),
        ],
        compiler_params=pltpu.CompilerParams(
            collective_id=0, has_side_effects=True, vmem_limit_bytes=56 * 1024 * 1024
        ),
    )(tokens, expert_ids, gate_weights, placement, w_gate[0], w_up[0], w_down[0])


def solution(mesh):
    placed = (
        P(("groups", "expert", "dp"), None),
        P(("groups", "expert", "dp"), None),
        P(("groups", "expert", "dp"), None),
        P("groups", None),
        P("expert", "dp", None),
        P("expert", "dp", None),
        P("expert", "dp", None),
    )
    return jax.shard_map(
        body,
        mesh=mesh,
        in_specs=placed,
        out_specs=P(("groups", "expert", "dp"), None),
        check_vma=False,
    )
```

time: 122 us -> 42 us (0.34)
  waiting for transfers between devices: 44.9 us -> 0 us
  Pallas kernels: 0 us -> 37.7 us
  blocking collectives: 32.7 us -> 0 us
  between operations: 14.1 us -> 0.01 us
  starting transfers between devices: 9.52 us -> 0 us
  matrix products: 7.95 us -> 0 us
  local copies, waits for them, and re-layouts: 8.28 us -> 4.03 us
  other arithmetic: 3.84 us -> 0 us
    pallas_call x0 -> x1, Pallas kernels: none -> 37.7 us  [body(): pl.pallas_call(functools.partial(kernel, experts, dp, topk, first, slots,...]
    all_gather x3 -> x0, blocking collectives: 25.4 us -> none  [the longest x1 9.95 us: body(): group_ids = lax.all_gather(expert_ids, 'dp', axis=0, tiled=True)]
    reduce_scatter x1 -> x0, waiting for transfers between devices: 24.9 us -> none  [body(): lax.psum_scatter(partial_value.astype(jnp.float32).astype(jnp.bfloat16),...]
    all_to_all x2 -> x0, waiting for transfers between devices: 20 us -> none  [the longest x1 13.4 us: body(): lax.all_to_all(send.reshape(experts, slots, width), 'expert', split_axis=...]
    all_to_all x2 -> x0, starting transfers between devices: 9.49 us -> none  [the longest x1 4.88 us: body(): lax.all_to_all(send.reshape(experts, slots, width), 'expert', split_axis=...]
    dot_general x4 -> x0, matrix products: 7.95 us -> none  [the longest x1 5.59 us: expert_block(): jnp.dot(hidden, down_w, preferred_element_type=jnp.float32)]
    all_to_all x1 -> x0, blocking collectives: 7.3 us -> none  [body(): lax.all_to_all(group_cols.astype(jnp.bfloat16), 'dp', split_axis=0, conca...]
    reshape x5 -> x0, local copies, waits for them, and re-layouts: 3.77 us -> none  [the longest x1 1.05 us: body(): main.reshape(experts, first, width)]
  transfers between devices with their start and end apart: 3 -> 0, of which waited for: 3 -> 0; matrix products, arithmetic and copies ran while one was open for 1% -> 0% of each run, Pallas kernels for 0% -> 0%
where the time goes in v1:
time: 42 us; the launch traced here: 41.7 us
  Pallas kernels  37.7 us (90%)
  local copies, waits for them, and re-layouts  4.03 us (10%)
    pallas_call x1, Pallas kernels, body(): pl.pallas_call(functools.partial(kernel, experts, dp, topk, first, slots,...  37.7 us
    unnamed x3, local copies, waits for them, and re-layouts  4.03 us

profile of v1, /device:TPU:0, one launch (start us, length us, event | category | flops | bytes accessed | tf_op | source)
XLA Modules:
  0.0 41.7 jit_solution(16075652073286431625)
XLA Ops:
  0.0 1.3 %copy.9.gates = bf16[4,2]{1,0:T(4,128)(2,1)} copy(bf16[4,2]{0,1:T(2,128)(2,1)} %param.9) | data formatting | bytes 32 | tf_op args[2]
  1.3 1.3 %copy.8.ids = s32[4,2]{1,0:T(4,128)} copy(s32[4,2]{0,1:T(2,128)} %param.8) | data formatting | bytes 64 | tf_op args[1]
  2.6 37.7 %shard_map.73 = bf16[4,4096]{1,0:T(4,128)(2,1)} custom-call(bf16[4,4096]{1,0:T(4,128)(2,1)} %tok.1, s32[4,2]{1,0:T(4,128)} %copy.8.ids, bf16[4,2]{1,0:T(4,128)(2,1)} %copy.9.gates, s32[2,2]{1,0:T(2,128)} %placement.1, bf16[384,4096]{1,0:T(8,128)(2,1)} %bitcast.3, bf16[384,4096]{1,0:T(8,128)(2,1)} %bitcast.4, bf16[384,4096]{1,0:T(8,128)(2,1)} %bitcast.5), custom_call_target="tpu_custom_call" | custom-call | tf_op jit(solution)/shard_map/pallas_call | solution.py:258
  40.3 1.4 %copy.11 = bf16[4,4096]{1,0:T(4,128)(2,1)} copy(bf16[4,4096]{1,0:T(4,128)(2,1)} %shard_map.73) | data formatting | bytes 65536

commit v2 on v1

--- a/solution.py
+++ b/solution.py
@@ -29,7 +29,8 @@
 
 
 def kernel(experts, dp, topk, first, slots, padded,
-           tok, ids, gates, placement, wg_hbm, wu_hbm, wd_hbm, out,
+           tok_hbm, ids_hbm, gates_hbm, placement_hbm, wg_hbm, wu_hbm, wd_hbm, out,
+           tok, ids, gates, placement,
            wg, wu, wd, tok_s, tok_r, info_s, info_r, group_x, disp_s, rows_r, rows_f, part_f,
            part_s, part_r, back_s, back_r, wsel, mix_s, mix_r,
            w_sem, s1, r1, si, ri, s2, r2, s3, r3, s4, r4, s5, r5, s6, r6):
@@ -42,11 +43,6 @@
     lanes = info_s.shape[1]
     total = experts * padded
 
-    loads = [pltpu.make_async_copy(a, b, w_sem.at[i])
-             for i, (a, b) in enumerate(((wg_hbm, wg), (wu_hbm, wu), (wd_hbm, wd)))]
-    for load in loads:
-        load.start()
-
     def to_dp(src, dst, send, recv, shift):
         return pltpu.make_async_remote_copy(
             src_ref=src, dst_ref=dst, send_sem=send, recv_sem=recv,
@@ -68,6 +64,15 @@
         pl.semaphore_signal(barrier, inc=1, device_id={"expert": lax.rem(me_e + d, experts)}, device_id_type=MESH)
 
     each_from(1, experts, greet)
+
+    pairs_of = ((ids_hbm, ids), (gates_hbm, gates), (placement_hbm, placement), (tok_hbm, tok),
+                (wg_hbm, wg), (wu_hbm, wu), (wd_hbm, wd))
+    loads = [pltpu.make_async_copy(a, b, w_sem.at[i]) for i, (a, b) in enumerate(pairs_of)]
+    for load in loads:
+        load.start()
+    for load in loads[:4]:
+        load.wait()
+    loads = loads[4:]
 
     lane = lax.broadcasted_iota(jnp.int32, (8, lanes), 1)
     line = lax.broadcasted_iota(jnp.int32, (8, lanes), 0)
@@ -77,8 +82,8 @@
     for t in range(own):
         for k in range(topk):
             here = lane == (me_j * own + t) * topk + k
-            value = jnp.where(line == 0, jnp.broadcast_to(id_f[t:t + 1, k:k + 1], (8, lanes)),
-                              jnp.broadcast_to(gate_f[t:t + 1, k:k + 1], (8, lanes)))
+            value = jnp.where(line == 0, jnp.broadcast_to(id_f[k:k + 1, t:t + 1], (8, lanes)),
+                              jnp.broadcast_to(gate_f[k:k + 1, t:t + 1], (8, lanes)))
             info = jnp.where(here, value, info)
     info_s[...] = info
     for s in range(1, dp):
@@ -104,8 +109,9 @@
     same = jnp.broadcast_to(id_col, (pairs, lanes)) == jnp.broadcast_to(id_row, (pairs, lanes))
     rank = jnp.sum(jnp.where(same, jnp.where(at_row < at_lane, 1.0, 0.0), 0.0), axis=0, keepdims=True)
     limit = jnp.full((1, lanes), float(first), F32)
+    listed = placement[...].astype(F32)
     for h in range(placement.shape[1]):
-        limit = jnp.where(id_row == placement[0, h].astype(F32), float(slots), limit)
+        limit = jnp.where(id_row == jnp.broadcast_to(listed[0:1, h:h + 1], (1, lanes)), float(slots), limit)
     dest = jnp.where(rank < limit, id_row * float(padded) + rank, -1.0)
     dest = jnp.where(lax.broadcasted_iota(jnp.int32, (1, lanes), 1) < pairs, dest, -1.0)
     pick = lax.broadcasted_iota(jnp.int32, (total, lanes), 0).astype(F32) == jnp.broadcast_to(dest, (total, lanes))
@@ -113,8 +119,6 @@
     token_i = lax.broadcasted_iota(jnp.int32, (lanes, group), 1) * topk
     fold = jnp.where(pair_i >= token_i, jnp.where(pair_i < token_i + topk, 1.0, 0.0), 0.0).astype(BF16)
     select = jnp.dot(jnp.where(pick, 1.0, 0.0).astype(BF16), fold, preferred_element_type=F32).astype(BF16)
-    wsel[...] = jnp.dot(jnp.where(pick, jnp.broadcast_to(gate_row, (total, lanes)), 0.0).astype(BF16), fold,
-                        preferred_element_type=F32)
 
     for s in range(1, dp):
         to_dp(tok_s.at[s], tok_r.at[lax.rem(me_j + dp - s, dp)], s1.at[s], r1.at[s], s).wait_recv()
@@ -137,6 +141,9 @@
             to_dp(rows_r.at[me_j, g], rows_r.at[me_j, g], s3.at[s, d], r3.at[s, d], s).start()
 
     forward(0)
+    wsel[...] = jnp.dot(jnp.where(pick, jnp.broadcast_to(gate_row, (total, lanes)), 0.0).astype(BF16), fold,
+                        preferred_element_type=F32)
+
 
     def arrive(d):
         g = lax.rem(me_e + experts - d, experts)
@@ -172,16 +179,20 @@
         part_f[...] = jnp.dot(hidden, wd[:, cols(j)], preferred_element_type=F32)
         target = part_s if s > 0 else part_r
 
-        def split(g):
-            target[s, g] = part_f[pl.ds(g * padded, slots), :].astype(BF16)
-
-        each(experts, split)
-        if s > 0:
-            to_dp(part_s.at[s], part_r.at[s], s4.at[s], r4.at[s], s).start()
-    for s in range(1, dp):
-        to_dp(part_s.at[s], part_r.at[s], s4.at[s], r4.at[s], s).wait_recv()
-
-    def summed(g):
+        def split(d):
+            g = lax.rem(me_e + d, experts)
+            start = pl.multiple_of(g * padded, 8)
+            target[s, g] = part_f[pl.ds(start, slots), :].astype(BF16)
+            if s > 0:
+                to_dp(part_s.at[s, g], part_r.at[s, g], s4.at[s, d], r4.at[s, d], s).start()
+
+        each_from(1, experts, split)
+        split(0)
+
+    def summed(d):
+        g = lax.rem(me_e + d, experts)
+        for s in range(1, dp):
+            to_dp(part_s.at[s, g], part_r.at[s, g], s4.at[s, d], r4.at[s, d], s).wait_recv()
         value = part_r[0, g].astype(F32)
         for s in range(1, dp):
             value = value + part_r[s, g].astype(F32)
@@ -189,11 +200,11 @@
 
     def give(d):
         g = lax.rem(me_e + d, experts)
-        back_s[g] = summed(g)
+        back_s[g] = summed(d)
         to_expert(back_s.at[g], back_r.at[me_e], s5.at[d], r5.at[d], d).start()
 
     each_from(1, experts, give)
-    back_r[me_e] = summed(me_e)
+    back_r[me_e] = summed(0)
 
     def collect(d):
         e = lax.rem(me_e + experts - d, experts)
@@ -221,13 +232,13 @@
     for s in range(1, dp):
         to_dp(info_s, info_r.at[s], si.at[s], ri.at[s], s).wait_send()
         to_dp(tok_s.at[s], tok_r.at[me_j], s1.at[s], r1.at[s], s).wait_send()
-        to_dp(part_s.at[s], part_r.at[s], s4.at[s], r4.at[s], s).wait_send()
         to_dp(mix_s.at[lax.rem(me_j + s, dp)], mix_r.at[me_j], s6.at[s], r6.at[s], s).wait_send()
 
     def left(d):
         g = lax.rem(me_e + experts - d, experts)
         for s in range(1, dp):
             to_dp(rows_r.at[me_j, g], rows_r.at[me_j, g], s3.at[s, d], r3.at[s, d], s).wait_send()
+            to_dp(part_s.at[s, g], part_r.at[s, g], s4.at[s, d], r4.at[s, d], s).wait_send()
 
     def left_expert(d):
         e = lax.rem(me_e + d, experts)
@@ -252,15 +263,18 @@
     units = w_gate.shape[1]
     total = experts * padded
     vmem = pl.BlockSpec(memory_space=pltpu.VMEM)
-    smem = pl.BlockSpec(memory_space=pltpu.SMEM)
     hbm = pl.BlockSpec(memory_space=pl.ANY)
     dma = pltpu.SemaphoreType.DMA
     return pl.pallas_call(
         functools.partial(kernel, experts, dp, topk, first, slots, padded),
         out_shape=jax.ShapeDtypeStruct((own, width), BF16),
-        in_specs=[vmem, vmem, vmem, smem, hbm, hbm, hbm],
+        in_specs=[hbm] * 7,
         out_specs=vmem,
         scratch_shapes=[
+            pltpu.VMEM((own, width), BF16),
+            pltpu.VMEM((topk, own), jnp.int32),
+            pltpu.VMEM((topk, own), BF16),
+            pltpu.VMEM(placement.shape, jnp.int32),
             pltpu.VMEM((units, width), BF16),
             pltpu.VMEM((units, width), BF16),
             pltpu.VMEM((units, width), BF16),
@@ -280,18 +294,18 @@
             pltpu.VMEM((total, group), F32),
             pltpu.VMEM((dp, own, block), BF16),
             pltpu.VMEM((dp, own, block), BF16),
-            dma((3,)),
+            dma((7,)),
             dma((dp,)), dma((dp,)), dma((dp,)), dma((dp,)),
             dma((experts,)), dma((experts,)),
             dma((dp, experts)), dma((dp, experts)),
-            dma((dp,)), dma((dp,)),
+            dma((dp, experts)), dma((dp, experts)),
             dma((experts,)), dma((experts,)),
             dma((dp,)), dma((dp,)),
         ],
         compiler_params=pltpu.CompilerParams(
-            collective_id=0, has_side_effects=True, vmem_limit_bytes=56 * 1024 * 1024
+            collective_id=0, has_side_effects=True, vmem_limit_bytes=56 << 20
         ),
-    )(tokens, expert_ids, gate_weights, placement, w_gate[0], w_up[0], w_down[0])
+    )(tokens, expert_ids.T, gate_weights.T, placement, w_gate[0], w_up[0], w_down[0])
 
 
 def solution(mesh):

time: 42 us -> 37.7 us (0.90)
  local copies, waits for them, and re-layouts: 4.03 us -> 1.39 us
  Pallas kernels: 37.7 us -> 36.2 us
    unnamed x3 -> x1, local copies, waits for them, and re-layouts: 4.03 us -> 1.39 us
    pallas_call x1, Pallas kernels: 37.7 us -> 36.2 us  [body(): pl.pallas_call(functools.partial(kernel, experts, dp, topk, first, slots,...]
where the time goes in v2:
time: 37.7 us; the launch traced here: 37.5 us
  Pallas kernels  36.2 us (96%)
  local copies, waits for them, and re-layouts  1.39 us (4%)
    pallas_call x1, Pallas kernels, body(): pl.pallas_call(functools.partial(kernel, experts, dp, topk, first, slots,...  36.2 us
    unnamed x1, local copies, waits for them, and re-layouts  1.39 us

profile of v2, /device:TPU:0, one launch (start us, length us, event | category | flops | bytes accessed | tf_op | source)
XLA Modules:
  0.0 37.5 jit_solution(16284432199661649899)
XLA Ops:
  0.0 36.2 %shard_map.73 = bf16[4,4096]{1,0:T(4,128)(2,1)} custom-call(bf16[4,4096]{1,0:T(4,128)(2,1)} %tok_hbm.1, s32[2,4]{1,0:T(2,128)} %bitcast.8, bf16[2,4]{1,0:T(2,128)(2,1)} %bitcast.9, s32[2,2]{1,0:T(2,128)} %placement_hbm.1, bf16[384,4096]{1,0:T(8,128)(2,1)} %bitcast.5, bf16[384,4096]{1,0:T(8,128)(2,1)} %bitcast.6, bf16[384,4096]{1,0:T(8,128)(2,1)} %bitcast.7), custom_call_target="tpu_custom_call" | custom-call | tf_op jit(solution)/shard_map/pallas_call | solution.py:268
  36.2 1.4 %copy.9 = bf16[4,4096]{1,0:T(4,128)(2,1)} copy(bf16[4,4096]{1,0:T(4,128)(2,1)} %shard_map.73) | data formatting | bytes 65536

commit v3 on v2

--- a/solution.py
+++ b/solution.py
@@ -32,7 +32,7 @@
            tok_hbm, ids_hbm, gates_hbm, placement_hbm, wg_hbm, wu_hbm, wd_hbm, out,
            tok, ids, gates, placement,
            wg, wu, wd, tok_s, tok_r, info_s, info_r, group_x, disp_s, rows_r, rows_f, part_f,
-           part_s, part_r, back_s, back_r, wsel, mix_s, mix_r,
+           part_s, part_r, back_s, back_r, wsel, mix_s,
            w_sem, s1, r1, si, ri, s2, r2, s3, r3, s4, r4, s5, r5, s6, r6):
     me_e = lax.axis_index("expert")
     me_j = lax.axis_index("dp")
@@ -43,10 +43,18 @@
     lanes = info_s.shape[1]
     total = experts * padded
 
-    def to_dp(src, dst, send, recv, shift):
+    if dp == 4:
+        low, high = lax.rem(me_j, 2), me_j // 2
+        across = (me_j, high * 2 + (1 - low), (1 - high) * 2 + low, (1 - high) * 2 + (1 - low))
+        onward = backward = lambda s: across[s]
+    else:
+        onward = lambda s: lax.rem(me_j + s, dp)
+        backward = lambda s: lax.rem(me_j + dp - s, dp)
+
+    def to_dp(src, dst, send, recv, s):
         return pltpu.make_async_remote_copy(
             src_ref=src, dst_ref=dst, send_sem=send, recv_sem=recv,
-            device_id={"dp": lax.rem(me_j + shift, dp)}, device_id_type=MESH)
+            device_id={"dp": onward(s)}, device_id_type=MESH)
 
     def to_expert(src, dst, send, recv, shift):
         return pltpu.make_async_remote_copy(
@@ -58,7 +66,7 @@
 
     barrier = pltpu.get_barrier_semaphore()
     for s in range(1, dp):
-        pl.semaphore_signal(barrier, inc=1, device_id={"dp": lax.rem(me_j + s, dp)}, device_id_type=MESH)
+        pl.semaphore_signal(barrier, inc=1, device_id={"dp": onward(s)}, device_id_type=MESH)
 
     def greet(d):
         pl.semaphore_signal(barrier, inc=1, device_id={"expert": lax.rem(me_e + d, experts)}, device_id_type=MESH)
@@ -87,7 +95,7 @@
             info = jnp.where(here, value, info)
     info_s[...] = info
     for s in range(1, dp):
-        tok_s[s] = tok[:, cols(lax.rem(me_j + s, dp))]
+        tok_s[s] = tok[:, cols(onward(s))]
     tok_r[me_j] = tok[:, cols(me_j)]
 
     pl.semaphore_wait(barrier, dp - 1 + experts - 1)
@@ -121,7 +129,7 @@
     select = jnp.dot(jnp.where(pick, 1.0, 0.0).astype(BF16), fold, preferred_element_type=F32).astype(BF16)
 
     for s in range(1, dp):
-        to_dp(tok_s.at[s], tok_r.at[lax.rem(me_j + dp - s, dp)], s1.at[s], r1.at[s], s).wait_recv()
+        to_dp(tok_s.at[s], tok_r.at[backward(s)], s1.at[s], r1.at[s], s).wait_recv()
     for j in range(dp):
         group_x[j * own:(j + 1) * own, :] = tok_r[j].astype(F32)
     rows_f[...] = jnp.dot(select, group_x[...].astype(BF16), preferred_element_type=F32)
@@ -135,9 +143,12 @@
     each_from(1, experts, dispatch)
     rows_r[me_j, me_e] = rows_f[pl.ds(pl.multiple_of(me_e * padded, 8), slots), :].astype(BF16)
 
+    relayed = dp == 4 and experts <= 8
+    direct = (1, 2) if relayed else range(1, dp)
+
     def forward(d):
         g = lax.rem(me_e + experts - d, experts)
-        for s in range(1, dp):
+        for s in direct:
             to_dp(rows_r.at[me_j, g], rows_r.at[me_j, g], s3.at[s, d], r3.at[s, d], s).start()
 
     forward(0)
@@ -155,13 +166,24 @@
     loads[0].wait()
     loads[1].wait()
     contract = (((1,), (1,)), ((), ()))
+
+    def first_of(d):
+        return 1 + d % 2
+
+    def relay(d):
+        g = lax.rem(me_e + experts - d, experts)
+        side = first_of(d)
+        j = onward(side)
+        to_dp(rows_r.at[j, g], rows_r.at[j, g], s3.at[side, d], r3.at[side, d], side).wait_recv()
+        to_dp(rows_r.at[j, g], rows_r.at[j, g], s3.at[3, d], r3.at[3, d], 3 - side).start()
+
     gate = up = None
     for s in range(dp):
-        j = lax.rem(me_j + dp - s, dp)
+        j = backward(s)
 
         def take(d):
             g = lax.rem(me_e + experts - d, experts)
-            if s > 0:
+            if s > 0 and not (relayed and s == first_of(d)):
                 to_dp(rows_r.at[j, g], rows_r.at[j, g], s3.at[s, d], r3.at[s, d], s).wait_recv()
             rows_f[pl.ds(pl.multiple_of(g * padded, 8), slots), :] = rows_r[j, g].astype(F32)
 
@@ -171,11 +193,13 @@
         up_part = lax.dot_general(x, wu[:, cols(j)], contract, preferred_element_type=F32)
         gate = gate_part if gate is None else gate + gate_part
         up = up_part if up is None else up + up_part
+        if relayed and s == 0:
+            each(experts, relay)
     hidden = (gate / (1.0 + jnp.exp(-gate)) * up).astype(BF16)
 
     loads[2].wait()
-    for s in list(range(1, dp)) + [0]:
-        j = lax.rem(me_j + s, dp)
+    for s in reversed(range(dp)):
+        j = onward(s)
         part_f[...] = jnp.dot(hidden, wd[:, cols(j)], preferred_element_type=F32)
         target = part_s if s > 0 else part_r
 
@@ -220,19 +244,19 @@
                                    preferred_element_type=F32)
     for j in range(dp):
         mix_s[j] = group_x[j * own:(j + 1) * own, :].astype(BF16)
-    for s in range(1, dp):
-        to_dp(mix_s.at[lax.rem(me_j + s, dp)], mix_r.at[me_j], s6.at[s], r6.at[s], s).start()
-    mix_r[me_j] = mix_s[me_j]
-    for s in range(1, dp):
-        j = lax.rem(me_j + dp - s, dp)
-        to_dp(mix_s.at[j], mix_r.at[j], s6.at[s], r6.at[s], s).wait_recv()
-    for j in range(dp):
-        out[:, j * block:(j + 1) * block] = mix_r[j]
+    for s in reversed(range(1, dp)):
+        to_dp(mix_s.at[onward(s)], out.at[:, cols(me_j)], s6.at[s], r6.at[s], s).start()
+    kept = pltpu.make_async_copy(mix_s.at[me_j], out.at[:, cols(me_j)], s6.at[0])
+    kept.start()
+    kept.wait()
+    for s in range(1, dp):
+        j = backward(s)
+        to_dp(mix_s.at[j], out.at[:, cols(j)], s6.at[s], r6.at[s], s).wait_recv()
 
     for s in range(1, dp):
         to_dp(info_s, info_r.at[s], si.at[s], ri.at[s], s).wait_send()
         to_dp(tok_s.at[s], tok_r.at[me_j], s1.at[s], r1.at[s], s).wait_send()
-        to_dp(mix_s.at[lax.rem(me_j + s, dp)], mix_r.at[me_j], s6.at[s], r6.at[s], s).wait_send()
+        to_dp(mix_s.at[onward(s)], out.at[:, cols(me_j)], s6.at[s], r6.at[s], s).wait_send()
 
     def left(d):
         g = lax.rem(me_e + experts - d, experts)
@@ -262,14 +286,13 @@
     block = width // dp
     units = w_gate.shape[1]
     total = experts * padded
-    vmem = pl.BlockSpec(memory_space=pltpu.VMEM)
     hbm = pl.BlockSpec(memory_space=pl.ANY)
     dma = pltpu.SemaphoreType.DMA
     return pl.pallas_call(
         functools.partial(kernel, experts, dp, topk, first, slots, padded),
         out_shape=jax.ShapeDtypeStruct((own, width), BF16),
         in_specs=[hbm] * 7,
-        out_specs=vmem,
+        out_specs=hbm,
         scratch_shapes=[
             pltpu.VMEM((own, width), BF16),
             pltpu.VMEM((topk, own), jnp.int32),
@@ -293,7 +316,6 @@
             pltpu.VMEM((experts, slots, block), BF16),
             pltpu.VMEM((total, group), F32),
             pltpu.VMEM((dp, own, block), BF16),
-            pltpu.VMEM((dp, own, block), BF16),
             dma((7,)),
             dma((dp,)), dma((dp,)), dma((dp,)), dma((dp,)),
             dma((experts,)), dma((experts,)),

time: 37.7 us -> 36.4 us (0.966)
  Pallas kernels: 36.2 us -> 34.9 us
    pallas_call x1, Pallas kernels: 36.2 us -> 34.9 us  [body(): pl.pallas_call(functools.partial(kernel, experts, dp, topk, first, slots,...]
where the time goes in v3:
time: 36.4 us; the launch traced here: 36.3 us
  Pallas kernels  34.9 us (96%)
  local copies, waits for them, and re-layouts  1.39 us (4%)
    pallas_call x1, Pallas kernels, body(): pl.pallas_call(functools.partial(kernel, experts, dp, topk, first, slots,...  34.9 us
    unnamed x1, local copies, waits for them, and re-layouts  1.39 us

profile of v3, /device:TPU:0, one launch (start us, length us, event | category | flops | bytes accessed | tf_op | source)
XLA Modules:
  0.0 36.3 jit_solution(16238196882760517996)
XLA Ops:
  0.0 34.9 %shard_map.73 = bf16[4,4096]{1,0:T(4,128)(2,1)} custom-call(bf16[4,4096]{1,0:T(4,128)(2,1)} %tok_hbm.1, s32[2,4]{1,0:T(2,128)} %bitcast.8, bf16[2,4]{1,0:T(2,128)(2,1)} %bitcast.9, s32[2,2]{1,0:T(2,128)} %placement_hbm.1, bf16[384,4096]{1,0:T(8,128)(2,1)} %bitcast.5, bf16[384,4096]{1,0:T(8,128)(2,1)} %bitcast.6, bf16[384,4096]{1,0:T(8,128)(2,1)} %bitcast.7), custom_call_target="tpu_custom_call" | custom-call | tf_op jit(solution)/shard_map/pallas_call | solution.py:291
  34.9 1.4 %copy.9 = bf16[4,4096]{1,0:T(4,128)(2,1)} copy(bf16[4,4096]{1,0:T(4,128)(2,1)} %shard_map.73) | data formatting | bytes 65536
